TPU v7x, 256 devices: a whole 4x4x8 slice. The times are simulated.
256 devices in a mesh: chan: 128 (over x_lo, z, y, core), tm: 2 (over x_hi).
Axes of the slice: x: 4 (x_hi: 2, x_lo: 2; x = x_hi * 2 + x_lo), y: 4, z: 8, core: 2. Of those that a mesh axis runs over, the one named last changes fastest.
Arguments:
- records: bfloat16 [6, 2048, 16384], P('tm', None, 'chan'), may hold values from -600 to 600
- band_taps: float32 [64], replicated, may hold values from -0.75 to 0.75
- white_taps: float32 [16, 16384], P(None, 'chan'), may hold values from -1.5 to 1.5
- live_mask: int32 [16384], P('chan'), may hold values 0 or 1
- partners: int32 [6, 128], P(None, 'chan'), may hold values from 0 to 127, as said below
Outputs:
- correlations: float32 [6, 32, 16384, 128], P(None, 'tm', 'chan')
Inputs may be any that keep to these rules, and one draw needn't show every extreme that they name: In each round blocks are matched in pairs: partners[r, b] differs from b, partners[r, partners[r, b]] = b, and partners[r, b] - b equals d or -d modulo 128, with the same d in the finite set (1, 2, 4) for all blocks of the round. Over all rounds every block b is matched with b + 1, b - 1, b + 2, b - 2, b + 4 and b - 4 modulo 128, each once.
All inputs are finite; a program needn't handle non-finite values. No bound on the sum of `live_mask` on one device may be relied on, other than what follows from the above.
Results may differ from a plain program's by a relative error of at most 0.0058.
Values may be sent and summed in bfloat16 or wider, within the bound.
No kernel may reach another device: no remote copies, remote signals or barrier semaphores. Data moves between devices by JAX's collectives and lax.ppermute only.
A program may use at most 64 MiB of HBM per device.

v0:
```python
import math
import jax
import jax.numpy as jnp
from jax import lax
from jax.sharding import PartitionSpec as P

NB = 128
SEG = 6
LAGS = 32


def shifted(value, axis, steps):
    count = lax.axis_size(axis)
    pairs = [(source, (source + steps) % count) for source in range(count)]
    return lax.ppermute(value, axis, pairs)


def bin_numbers(samples, bin_count):
    return samples // 64 + samples // (4 * bin_count) * jnp.arange(bin_count, dtype=jnp.int32)


def rotation(products, samples):
    angles = jnp.mod(products, samples).astype(jnp.float32) * (2.0 * math.pi / samples)
    return (jnp.cos(angles), jnp.sin(angles))


def dft_table(samples, bin_index):
    sample_index = jnp.arange(samples, dtype=jnp.int32)
    cos_part, sin_part = rotation(sample_index[:, None] * bin_index[None, :], samples)
    return jnp.concatenate([cos_part, -sin_part], axis=1).astype(jnp.bfloat16)


def responses(band_taps, white_taps, bin_index, samples):
    highest = lax.Precision.HIGHEST
    band_cos, band_sin = rotation(
        jnp.arange(band_taps.shape[0], dtype=jnp.int32)[:, None] * bin_index[None, :], samples
    )
    white_cos, white_sin = rotation(
        jnp.arange(white_taps.shape[0], dtype=jnp.int32)[:, None] * bin_index[None, :], samples
    )
    band_real = jnp.dot(band_taps, band_cos, precision=highest)
    band_imag = -jnp.dot(band_taps, band_sin, precision=highest)
    white_real = jnp.dot(white_taps.T, white_cos, precision=highest)
    white_imag = -jnp.dot(white_taps.T, white_sin, precision=highest)
    resp_real = white_real * band_real[None, :] - white_imag * band_imag[None, :]
    resp_imag = white_real * band_imag[None, :] + white_imag * band_real[None, :]
    return (resp_real, resp_imag)


def filtered(raw_spec, resp_real, resp_imag, live_values):
    bin_count = resp_real.shape[1]
    spec_real = raw_spec[..., :bin_count]
    spec_imag = raw_spec[..., bin_count:]
    real_resp = resp_real[:, None, :]
    imag_resp = resp_imag[:, None, :]
    out_real = (real_resp * spec_real - imag_resp * spec_imag) * live_values[:, None, None]
    out_imag = (real_resp * spec_imag + imag_resp * spec_real) * live_values[:, None, None]
    return jnp.concatenate([out_real, out_imag], axis=2).astype(jnp.bfloat16)


def inverse_norms(flat_rows):
    values = flat_rows.astype(jnp.float32)
    mean_square = jnp.sum(values * values, axis=-1) / (SEG * NB)
    return lax.rsqrt(mean_square + 1e-06)


def turned_rows(own_block, lag_values, bin_index, samples):
    lag_cos, lag_sin = rotation(lag_values[:, None] * bin_index[None, :], samples)
    values = own_block.astype(jnp.float32).reshape(own_block.shape[0], SEG, 2, NB)
    part_real = values[:, :, 0, :][None]
    part_imag = values[:, :, 1, :][None]
    cos_factor = lag_cos[:, None, None, :]
    sin_factor = lag_sin[:, None, None, :]
    new_real = part_real * cos_factor - part_imag * sin_factor
    new_imag = part_real * sin_factor + part_imag * cos_factor
    stacked = jnp.stack([new_real, new_imag], axis=3)
    return stacked.astype(jnp.bfloat16).reshape(lag_values.shape[0] * own_block.shape[0], -1)


def tile_sums(turned, chosen, own_scale, part_scale, lag_count):
    rounds, row_count, inner_size = chosen.shape
    flat_rows = chosen.reshape(rounds * row_count, inner_size)
    tile_totals = lax.dot_general(
        turned, flat_rows, (((1,), (1,)), ((), ())), preferred_element_type=jnp.float32
    )
    tile_totals = tile_totals.reshape(lag_count, row_count, rounds, row_count)
    scaled = (
        tile_totals
        * own_scale[None, :, None, None]
        * part_scale[None, None, :, :]
        * (1.0 / math.sqrt(SEG * NB))
    )
    return jnp.transpose(scaled, (2, 0, 1, 3))


def local(records, band_taps, white_taps, live_mask, partners):
    samples = records.shape[1]
    channels = records.shape[2]
    bin_index = bin_numbers(samples, NB)
    transform = dft_table(samples, bin_index)
    resp_real, resp_imag = responses(band_taps, white_taps, bin_index, samples)
    live_values = live_mask.astype(jnp.float32)
    raw_spec = jnp.einsum(
        "stc,tf->csf",
        lax.all_gather(records, "tm", axis=0, tiled=True),
        transform,
        preferred_element_type=jnp.float32,
    )
    spectra = filtered(raw_spec, resp_real, resp_imag, live_values)
    own_block = spectra.reshape(channels, -1)
    my_block = lax.axis_index("chan")
    block_count = lax.axis_size("chan")
    offset_list = (-4, -2, -1, 1, 2, 4)
    pieces = {}
    for offset in (1, 2, 4, -1, -2, -4):
        pieces[offset] = shifted(own_block, "chan", -offset)
    window = jnp.stack([pieces[offset] for offset in offset_list])
    delta = jnp.mod(partners[:, 0] - my_block + block_count // 2, block_count) - block_count // 2
    slot_index = jnp.zeros_like(delta)
    for position, offset in enumerate(offset_list):
        slot_index = slot_index + position * (delta == offset).astype(jnp.int32)
    chosen = jnp.take(window, slot_index, axis=0)
    own_scale = inverse_norms(own_block)
    part_scale = inverse_norms(chosen)
    lag_count = LAGS // lax.axis_size("tm")
    lag_first = lax.axis_index("tm") * lag_count
    lag_values = 3 * (lag_first + jnp.arange(lag_count, dtype=jnp.int32) - LAGS // 2)
    turned = turned_rows(own_block, lag_values, bin_index, samples)
    return tile_sums(turned, chosen, own_scale, part_scale, lag_count)


def solution(mesh):
    return jax.shard_map(
        local,
        mesh=mesh,
        in_specs=(P("tm", None, "chan"), P(), P(None, "chan"), P("chan"), P(None, "chan")),
        out_specs=P(None, "tm", "chan", None),
        check_vma=False,
    )
```

profile of v0, /device:TPU:2, one launch (start us, length us, event | category | flops | bytes accessed | tf_op | source)
XLA Modules:
  0.0 153.6 jit_solution(10691760521809553635)
XLA Ops:
  6.5 0.7 all-gather.2.cloned.1.call-update
  7.9 0.7 and_bitcast_fusion
  8.6 0.9 convolution_bitcast_fusion.2
  9.6 0.9 fusion.5
  11.4 4.9 %cosine_convert_fusion = (bf16[2048,128]{0,1:T(8,128)(2,1)S(1)}, bf16[2048,128]{0,1:T(8,128)(2,1)S(1)}) fusion(s32[128]{0:T(128)S(1)} %multiply_add_fusion), kind=kLoop, calls=%fused_computation.25 | loop fusion | flops 4456448 | bytes 1049088 | tf_op jit(solution)/shard_map/convert.3
  16.2 46.5 %all-gather.2.cloned.1.call-done = bf16[6,2048,128]{2,1,0:T(8,128)(2,1)} async-done(((bf16[3,2048,128]{2,1,0:T(8,128)(2,1)}), bf16[6,2048,128]{2,1,0:T(8,128)(2,1)}) %all-gather.2.cloned.1.call-update) | async-done | bytes 3145744 | tf_op jit(solution)/shard_map/all_gather | solution.py:105
  62.8 2.9 %convolution_bitcast_fusion = f32[128,6,256]{0,2,1:T(8,128)S(1)} fusion(bf16[6,2048,128]{2,1,0:T(8,128)(2,1)} %all-gather.2.cloned.1.call-done, bf16[2048,128]{0,1:T(8,128)(2,1)S(1)} %get-tuple-element.20, bf16[2048,128]{0,1:T(8,128)(2,1)S(1)} %get-tuple-element.19), kind=kOutput, calls=%fused_computation.13 | convolution fusion | flops 807403520 | bytes 4980736 | tf_op jit(solution)/shard_map/stc,tf->csf/dot_general | solution.py:103
  66.2 3.1 %collective-permute-start = (bf16[128,1536]{1,0:T(8,128)(2,1)S(1)}, bf16[128,1536]{1,0:T(8,128)(2,1)}, u32[]{:S(2)}, u32[]{:S(2)}) collective-permute-start(bf16[128,1536]{1,0:T(8,128)(2,1)S(1)} %copy.20), channel_id=1, source_target_pairs={{0,8},{2,10},{4,12},{6,14},{8,16},{10,18},{12,20},{14,22},{16,24},... | collective-permute-start | bytes 1179656 | tf_op jit(solution)/shard_map/ppermute | solution.py:15
  69.9 6.0 %collective-permute-start.3 = (bf16[128,1536]{1,0:T(8,128)(2,1)S(1)}, bf16[128,1536]{1,0:T(8,128)(2,1)S(1)}, u32[]{:S(2)}, u32[]{:S(2)}) collective-permute-start(bf16[128,1536]{1,0:T(8,128)(2,1)S(1)} %copy.20), channel_id=1, source_target_pairs={{0,254},{2,0},{4,2},{6,4},{8,6},{10,8},{12,10},{14,12},{16,14},{18... | collective-permute-start | bytes 1179656 | tf_op jit(solution)/shard_map/ppermute | solution.py:15
  75.8 1.4 collective-permute-start.4
  77.9 13.2 %subtract_convert_fusion = (bf16[16,128,6,1,128]{4,3,2,1,0:T(2,128)(2,1)S(1)}, bf16[16,128,6,1,128]{4,3,2,1,0:T(2,128)(2,1)S(1)}) fusion(f32[16,128]{1,0:T(8,128)S(1)} %get-tuple-element.18, f32[128,6,128]{2,1,0:T(8,128)S(1)} %copy.19, f32[16,128]{1,0:T(8,128)S(1)} %get-tuple-element.17, f32[128,6,128]{2,1,0:T(8,128)S(1)} %copy.18), kind=kLoop, calls=%fused_computation.6 | loop fusion | flops 12582912 | bytes 7094272 | tf_op jit(solution)/shard_map/convert.1
  91.1 15.4 %pad_maximum_fusion = bf16[16,128,6,2,128]{4,3,2,1,0:T(2,128)(2,1)} fusion(bf16[16,128,6,1,128]{4,3,2,1,0:T(2,128)(2,1)S(1)} %get-tuple-element.10, bf16[16,128,6,1,128]{4,3,2,1,0:T(2,128)(2,1)S(1)} %get-tuple-element.9), kind=kLoop, calls=%fused_computation.1 | loop fusion | flops 12582912 | bytes 12582912 | tf_op jit(solution)/shard_map/stack | solution.py:76
  106.5 14.4 %reshape.152 = bf16[16,128,1536,1]{2,1,0,3:T(8,128)(2,1)} reshape(bf16[16,128,6,2,128]{4,3,2,1,0:T(2,128)(2,1)} %pad_maximum_fusion) | data formatting | bytes 12582912 | tf_op jit(solution)/shard_map/convert_element_type | solution.py:77
  121.2 1.8 %bitcast_dynamic-update-slice_fusion.5 = bf16[6,128,1536]{2,1,0:T(8,128)(2,1)} fusion(bf16[128,1536]{1,0:T(8,128)(2,1)} %collective-permute-done), kind=kLoop, calls=%fused_computation.38 | loop fusion | bytes 786432
  123.0 0.8 bitcast_dynamic-update-slice_fusion.4
  123.8 0.8 bitcast_dynamic-update-slice_fusion.3
  124.6 0.8 bitcast_dynamic-update-slice_fusion.2
  125.3 0.8 bitcast_dynamic-update-slice_fusion.1
  126.1 6.3 %collective-permute-done.5 = bf16[128,1536]{1,0:T(8,128)(2,1)S(1)} collective-permute-done((bf16[128,1536]{1,0:T(8,128)(2,1)S(1)}, bf16[128,1536]{1,0:T(8,128)(2,1)S(1)}, u32[]{:S(2)}, u32[]{:S(2)}) %collective-permute-start.5) | collective-permute-done | bytes 393248 | tf_op jit(solution)/shard_map/ppermute | solution.py:15
  132.4 0.8 bitcast_dynamic-update-slice_fusion
  133.2 2.4 %gather_fusion = bf16[6,128,1536]{2,1,0:T(8,128)(2,1)S(1)} fusion(bf16[6,128,1536]{2,1,0:T(8,128)(2,1)} %bitcast_dynamic-update-slice_fusion, s32[1024]{0:T(1024)S(1)} %pad_clamp_fusion), kind=kCustom, calls=%fused_computation | custom fusion | bytes 4718616 | tf_op jit(solution)/shard_map/jit(_take)/gather | solution.py:122
  135.5 0.8 multiply_reduce_fusion
  136.3 7.4 %multiply_bitcast_fusion = f32[6,16,128,128]{3,2,0,1:T(8,128)S(1)} fusion(f32[6,128]{1,0:T(8,128)S(1)} %add_rsqrt_fusion, f32[128]{0:T(128)S(1)} %add_rsqrt_fusion.1, bf16[16,128,1536,1]{2,1,0,3:T(8,128)(2,1)} %reshape.152, bf16[6,128,1536]{2,1,0:T(8,128)(2,1)S(1)} %gather_fusion, pred[6]{0:T(512)(128)(4,1)S(1)} %get-tuple-element.7), kind=kOutput, calls=%fused_computation.4 | convolution fusion | flops 4837736448 | bytes 14945798 | tf_op jit(solution)/shard_map/dot_general | solution.py:83
  143.7 3.1 %copy.26 = f32[6,16,128,128]{3,2,1,0:T(8,128)} copy(f32[6,16,128,128]{3,2,0,1:T(8,128)S(1)} %multiply_bitcast_fusion) | data formatting | bytes 12582912 | tf_op jit(solution)/shard_map/mul | solution.py:88
  (27 shorter events, 3.6 us)
Async XLA Ops:
  6.5 4.1 %copy-start = (f32[16,128]{1,0:T(8,128)S(1)}, f32[16,128]{1,0:T(8,128)}, u32[]{:S(2)}) copy-start(f32[16,128]{1,0:T(8,128)} %param.7) | copy-start | bytes 24580
  6.5 56.2 %all-gather.2.cloned.1.call-start = ((), (), s32[]{:S(2)}) async-start(), calls=%async_computation | async-start | bytes 4718592 | tf_op jit(solution)/shard_map/all_gather | solution.py:105
  66.2 54.7 %collective-permute-start = (bf16[128,1536]{1,0:T(8,128)(2,1)S(1)}, bf16[128,1536]{1,0:T(8,128)(2,1)}, u32[]{:S(2)}, u32[]{:S(2)}) collective-permute-start(bf16[128,1536]{1,0:T(8,128)(2,1)S(1)} %copy.20), channel_id=1, source_target_pairs={{0,8},{2,10},{4,12},{6,14},{8,16},{10,18},{12,20},{14,22},{16,24},... | collective-permute-start | bytes 1179656 | tf_op jit(solution)/shard_map/ppermute | solution.py:15
  69.3 53.7 %collective-permute-start.1 = (bf16[128,1536]{1,0:T(8,128)(2,1)S(1)}, bf16[128,1536]{1,0:T(8,128)(2,1)S(1)}, u32[]{:S(2)}, u32[]{:S(2)}) collective-permute-start(bf16[128,1536]{1,0:T(8,128)(2,1)S(1)} %copy.20), channel_id=1, source_target_pairs={{0,4},{2,6},{4,8},{6,10},{8,12},{10,14},{12,16},{14,18},{16,20},{1... | collective-permute-start | bytes 1179656 | tf_op jit(solution)/shard_map/ppermute | solution.py:15
  69.9 53.9 %collective-permute-start.2 = (bf16[128,1536]{1,0:T(8,128)(2,1)S(1)}, bf16[128,1536]{1,0:T(8,128)(2,1)S(1)}, u32[]{:S(2)}, u32[]{:S(2)}) collective-permute-start(bf16[128,1536]{1,0:T(8,128)(2,1)S(1)} %copy.20), channel_id=1, source_target_pairs={{0,2},{2,4},{4,6},{6,8},{8,10},{10,12},{12,14},{14,16},{16,18},{18... | collective-permute-start | bytes 1179656 | tf_op jit(solution)/shard_map/ppermute | solution.py:15
  69.9 54.7 %collective-permute-start.3 = (bf16[128,1536]{1,0:T(8,128)(2,1)S(1)}, bf16[128,1536]{1,0:T(8,128)(2,1)S(1)}, u32[]{:S(2)}, u32[]{:S(2)}) collective-permute-start(bf16[128,1536]{1,0:T(8,128)(2,1)S(1)} %copy.20), channel_id=1, source_target_pairs={{0,254},{2,0},{4,2},{6,4},{8,6},{10,8},{12,10},{14,12},{16,14},{18... | collective-permute-start | bytes 1179656 | tf_op jit(solution)/shard_map/ppermute | solution.py:15
  75.8 49.5 %collective-permute-start.4 = (bf16[128,1536]{1,0:T(8,128)(2,1)S(1)}, bf16[128,1536]{1,0:T(8,128)(2,1)S(1)}, u32[]{:S(2)}, u32[]{:S(2)}) collective-permute-start(bf16[128,1536]{1,0:T(8,128)(2,1)S(1)} %copy.20), channel_id=1, source_target_pairs={{0,252},{2,254},{4,0},{6,2},{8,4},{10,6},{12,8},{14,10},{16,12},{1... | collective-permute-start | bytes 1179656 | tf_op jit(solution)/shard_map/ppermute | solution.py:15
  120.9 11.5 %collective-permute-start.5 = (bf16[128,1536]{1,0:T(8,128)(2,1)S(1)}, bf16[128,1536]{1,0:T(8,128)(2,1)S(1)}, u32[]{:S(2)}, u32[]{:S(2)}) collective-permute-start(bf16[128,1536]{1,0:T(8,128)(2,1)S(1)} %copy.20), channel_id=1, source_target_pairs={{0,248},{2,250},{4,252},{6,254},{8,0},{10,2},{12,4},{14,6},{16,8},... | collective-permute-start | bytes 1179656 | tf_op jit(solution)/shard_map/ppermute | solution.py:15
Sparse Core Ops, SparseCore 0:
  9.2 53.5 all-gather.1
where the time goes:
time: 154 us
  waiting for transfers between devices  53.5 us (35%)
  other arithmetic  36.1 us (23%)
  local copies, waits for them, and re-layouts  26.2 us (17%)
  between operations  13.5 us (9%)
  matrix products  12.8 us (8%)
  starting transfers between devices  11.4 us (7%)
    all_gather x1, waiting for transfers between devices, local(): lax.all_gather(records, 'tm', axis=0, tiled=True)  46.5 us
    another operation x2, other arithmetic  18.1 us
    another operation x1, other arithmetic, turned_rows(): stacked = jnp.stack([new_real, new_imag], axis=3)  15.4 us
    convert_element_type x1, local copies, waits for them, and re-layouts, turned_rows(): stacked.astype(jnp.bfloat16)  14.4 us
    ppermute x6, starting transfers between devices, shifted(): return lax.ppermute(value, axis, pairs)  11.4 us
    dot_general x1, matrix products, tile_sums(): lax.dot_general(turned, flat_rows, (((1,), (1,)), ((), ())), preferred_el...  7.36 us
    ppermute x6, waiting for transfers between devices, shifted(): return lax.ppermute(value, axis, pairs)  6.29 us
    unnamed x7, local copies, waits for them, and re-layouts  4.86 us
  transfers between devices with their start and end apart: 7, of which 2 were waited for; matrix products, arithmetic and copies ran while one was open for 37% of the time, Pallas kernels for 0%

commit v1 on v0

--- a/solution.py
+++ b/solution.py
@@ -94,6 +94,12 @@
 
 
 def local(records, band_taps, white_taps, live_mask, partners):
+
+    def _lift_circles(page, row_axis):
+        return jnp.concatenate(
+            lax.all_to_all(jnp.stack(lax.axis_size(row_axis) * [page], axis=0), row_axis, 0, 0), 0
+        )
+
     samples = records.shape[1]
     channels = records.shape[2]
     bin_index = bin_numbers(samples, NB)
@@ -101,10 +107,7 @@
     resp_real, resp_imag = responses(band_taps, white_taps, bin_index, samples)
     live_values = live_mask.astype(jnp.float32)
     raw_spec = jnp.einsum(
-        "stc,tf->csf",
-        lax.all_gather(records, "tm", axis=0, tiled=True),
-        transform,
-        preferred_element_type=jnp.float32,
+        "stc,tf->csf", _lift_circles(records, "tm"), transform, preferred_element_type=jnp.float32
     )
     spectra = filtered(raw_spec, resp_real, resp_imag, live_values)
     own_block = spectra.reshape(channels, -1)

time: 154 us -> 130 us (0.84)
  waiting for transfers between devices: 53.5 us -> 35.2 us
  between operations: 13.5 us -> 0.21 us
  starting transfers between devices: 11.4 us -> 17.5 us
  other arithmetic: 36.1 us -> 39.5 us
  matrix products: 12.8 us -> 10.8 us
    all_gather x1 -> x0, waiting for transfers between devices: 46.5 us -> none  [local(): lax.all_gather(records, 'tm', axis=0, tiled=True)]
    all_to_all x0 -> x1, waiting for transfers between devices: none -> 30.6 us  [_lift_circles(): lax.all_to_all(jnp.stack(lax.axis_size(row_axis) * [page], axis=0), row_a...]
    another operation x2 -> x3, other arithmetic: 18.1 us -> 22.8 us
    all_to_all x0 -> x1, starting transfers between devices: none -> 4.08 us  [_lift_circles(): lax.all_to_all(jnp.stack(lax.axis_size(row_axis) * [page], axis=0), row_a...]
    ppermute x6, starting transfers between devices: 11.4 us -> 13.4 us  [shifted(): return lax.ppermute(value, axis, pairs)]
    ppermute x6, waiting for transfers between devices: 6.29 us -> 4.6 us  [shifted(): return lax.ppermute(value, axis, pairs)]
    unnamed x7 -> x13, local copies, waits for them, and re-layouts: 4.86 us -> 4.87 us
  transfers between devices with their start and end apart: 7 -> 7, of which waited for: 2 -> 2; matrix products, arithmetic and copies ran while one was open for 37% -> 43% of each run, Pallas kernels for 0% -> 0%
where the time goes in v1:
time: 130 us; the launch traced here: 129 us
  other arithmetic  39.5 us (30%)
  waiting for transfers between devices  35.2 us (27%)
  local copies, waits for them, and re-layouts  26.3 us (20%)
  starting transfers between devices  17.5 us (13%)
  matrix products  10.8 us (8%)
    all_to_all x1, waiting for transfers between devices, _lift_circles(): lax.all_to_all(jnp.stack(lax.axis_size(row_axis) * [page], axis=0), row_a...  30.6 us
    another operation x2, other arithmetic  18.9 us
    another operation x1, other arithmetic, turned_rows(): stacked = jnp.stack([new_real, new_imag], axis=3)  15.4 us
    convert_element_type x1, local copies, waits for them, and re-layouts, turned_rows(): stacked.astype(jnp.bfloat16)  14.4 us
    ppermute x6, starting transfers between devices, shifted(): return lax.ppermute(value, axis, pairs)  13.4 us
    dot_general x1, matrix products, tile_sums(): lax.dot_general(turned, flat_rows, (((1,), (1,)), ((), ())), preferred_el...  7.36 us
    unnamed x13, local copies, waits for them, and re-layouts  4.87 us
    ppermute x6, waiting for transfers between devices, shifted(): return lax.ppermute(value, axis, pairs)  4.6 us
  transfers between devices with their start and end apart: 7, of which 2 were waited for; matrix products, arithmetic and copies ran while one was open for 43% of the time, Pallas kernels for 0%

profile of v1, /device:TPU:2, one launch (start us, length us, event | category | flops | bytes accessed | tf_op | source)
XLA Modules:
  0.0 129.5 jit_solution(1346958241435718699)
XLA Ops:
  0.0 3.8 %pad_maximum_fusion.1 = bf16[2,3,2048,128]{3,2,1,0:T(8,128)(2,1)} fusion(bf16[1,3,2048,128]{3,2,1,0:T(8,128)(2,1)} %bitcast.61), kind=kLoop, calls=%fused_computation.8 | loop fusion | flops 1572864 | bytes 4718592 | tf_op jit(solution)/shard_map/stack | solution.py:100
  3.9 4.1 %all-to-all-start = ((bf16[2,3,2048,128]{3,2,1,0:T(8,128)(2,1)}), bf16[2,3,2048,128]{3,2,1,0:T(8,128)(2,1)S(1)}, u32[]{:S(2)}, u32[]{:S(2)}) async-start(bf16[2,3,2048,128]{3,2,1,0:T(8,128)(2,1)} %pad_maximum_fusion.1), calls=%async_computation | async-start | bytes 6291456 | tf_op jit(solution)/shard_map/all_to_all | solution.py:100
  9.5 5.7 %cosine_convert_fusion = (bf16[2048,128]{0,1:T(8,128)(2,1)}, bf16[2048,128]{0,1:T(8,128)(2,1)}) fusion(s32[128]{0:T(128)S(1)} %multiply_add_fusion), kind=kLoop, calls=%fused_computation.26 | loop fusion | flops 4456448 | bytes 1049088 | tf_op jit(solution)/shard_map/convert.3
  15.2 30.6 %all-to-all-done = bf16[2,3,2048,128]{3,2,1,0:T(8,128)(2,1)S(1)} async-done(((bf16[2,3,2048,128]{3,2,1,0:T(8,128)(2,1)}), bf16[2,3,2048,128]{3,2,1,0:T(8,128)(2,1)S(1)}, u32[]{:S(2)}, u32[]{:S(2)}) %all-to-all-start) | async-done | bytes 3145760 | tf_op jit(solution)/shard_map/all_to_all | solution.py:100
  45.8 2.2 %convolution_bitcast_fusion = f32[128,6,256]{0,2,1:T(8,128)S(1)} fusion(bf16[6,2048,128]{2,1,0:T(8,128)(2,1)S(1)} %bitcast.60, bf16[2048,128]{0,1:T(8,128)(2,1)} %get-tuple-element.20, bf16[2048,128]{0,1:T(8,128)(2,1)} %get-tuple-element.19), kind=kOutput, calls=%fused_computation.14 | convolution fusion | flops 807403520 | bytes 4980736 | tf_op jit(solution)/shard_map/stc,tf->csf/dot_general | solution.py:109
  48.5 3.3 %collective-permute-start = (bf16[128,1536]{1,0:T(8,128)(2,1)S(1)}, bf16[128,1536]{1,0:T(8,128)(2,1)}, u32[]{:S(2)}, u32[]{:S(2)}) collective-permute-start(bf16[128,1536]{1,0:T(8,128)(2,1)S(1)} %copy.11), channel_id=1, source_target_pairs={{0,8},{2,10},{4,12},{6,14},{8,16},{10,18},{12,20},{14,22},{16,24},... | collective-permute-start | bytes 1179656 | tf_op jit(solution)/shard_map/ppermute | solution.py:15
  51.8 0.7 collective-permute-start.1
  52.5 6.0 %collective-permute-start.3 = (bf16[128,1536]{1,0:T(8,128)(2,1)S(1)}, bf16[128,1536]{1,0:T(8,128)(2,1)S(1)}, u32[]{:S(2)}, u32[]{:S(2)}) collective-permute-start(bf16[128,1536]{1,0:T(8,128)(2,1)S(1)} %copy.11), channel_id=1, source_target_pairs={{0,254},{2,0},{4,2},{6,4},{8,6},{10,8},{12,10},{14,12},{16,14},{18... | collective-permute-start | bytes 1179656 | tf_op jit(solution)/shard_map/ppermute | solution.py:15
  58.5 1.3 %collective-permute-start.4 = (bf16[128,1536]{1,0:T(8,128)(2,1)S(1)}, bf16[128,1536]{1,0:T(8,128)(2,1)S(1)}, u32[]{:S(2)}, u32[]{:S(2)}) collective-permute-start(bf16[128,1536]{1,0:T(8,128)(2,1)S(1)} %copy.11), channel_id=1, source_target_pairs={{0,252},{2,254},{4,0},{6,2},{8,4},{10,6},{12,8},{14,10},{16,12},{1... | collective-permute-start | bytes 1179656 | tf_op jit(solution)/shard_map/ppermute | solution.py:15
  60.4 13.2 %subtract_convert_fusion = (bf16[16,128,6,1,128]{4,3,2,1,0:T(2,128)(2,1)S(1)}, bf16[16,128,6,1,128]{4,3,2,1,0:T(2,128)(2,1)S(1)}) fusion(f32[16,128]{1,0:T(8,128)S(1)} %get-tuple-element.18, f32[128,6,128]{2,1,0:T(8,128)S(1)} %copy.10, f32[16,128]{1,0:T(8,128)S(1)} %get-tuple-element.17, f32[128,6,128]{2,1,0:T(8,128)S(1)} %copy.9), kind=kLoop, calls=%fused_computation.6 | loop fusion | flops 12582912 | bytes 7094272 | tf_op jit(solution)/shard_map/convert.1
  73.7 15.4 %pad_maximum_fusion = bf16[16,128,6,2,128]{4,3,2,1,0:T(2,128)(2,1)} fusion(bf16[16,128,6,1,128]{4,3,2,1,0:T(2,128)(2,1)S(1)} %get-tuple-element.10, bf16[16,128,6,1,128]{4,3,2,1,0:T(2,128)(2,1)S(1)} %get-tuple-element.9), kind=kLoop, calls=%fused_computation.1 | loop fusion | flops 12582912 | bytes 12582912 | tf_op jit(solution)/shard_map/stack | solution.py:76
  89.0 14.4 %reshape.156 = bf16[16,128,1536,1]{2,1,0,3:T(8,128)(2,1)} reshape(bf16[16,128,6,2,128]{4,3,2,1,0:T(2,128)(2,1)} %pad_maximum_fusion) | data formatting | bytes 12582912 | tf_op jit(solution)/shard_map/convert_element_type | solution.py:77
  103.5 2.1 %collective-permute-start.5 = (bf16[128,1536]{1,0:T(8,128)(2,1)S(1)}, bf16[128,1536]{1,0:T(8,128)(2,1)S(1)}, u32[]{:S(2)}, u32[]{:S(2)}) collective-permute-start(bf16[128,1536]{1,0:T(8,128)(2,1)S(1)} %copy.11), channel_id=1, source_target_pairs={{0,248},{2,250},{4,252},{6,254},{8,0},{10,2},{12,4},{14,6},{16,8},... | collective-permute-start | bytes 1179656 | tf_op jit(solution)/shard_map/ppermute | solution.py:15
  105.6 1.8 %bitcast_dynamic-update-slice_fusion.5 = bf16[6,128,1536]{2,1,0:T(8,128)(2,1)} fusion(bf16[128,1536]{1,0:T(8,128)(2,1)} %collective-permute-done), kind=kLoop, calls=%fused_computation.39 | loop fusion | bytes 786432
  107.4 0.8 bitcast_dynamic-update-slice_fusion.4
  108.1 0.8 bitcast_dynamic-update-slice_fusion.3
  108.9 0.8 bitcast_dynamic-update-slice_fusion.2
  109.7 0.8 bitcast_dynamic-update-slice_fusion.1
  110.5 4.6 %collective-permute-done.5 = bf16[128,1536]{1,0:T(8,128)(2,1)S(1)} collective-permute-done((bf16[128,1536]{1,0:T(8,128)(2,1)S(1)}, bf16[128,1536]{1,0:T(8,128)(2,1)S(1)}, u32[]{:S(2)}, u32[]{:S(2)}) %collective-permute-start.5) | collective-permute-done | bytes 393248 | tf_op jit(solution)/shard_map/ppermute | solution.py:15
  115.0 0.8 bitcast_dynamic-update-slice_fusion
  115.8 2.4 %gather_fusion = bf16[6,128,1536]{2,1,0:T(8,128)(2,1)S(1)} fusion(bf16[6,128,1536]{2,1,0:T(8,128)(2,1)} %bitcast_dynamic-update-slice_fusion, s32[1024]{0:T(1024)S(1)} %pad_clamp_fusion), kind=kCustom, calls=%fused_computation | custom fusion | bytes 4718616 | tf_op jit(solution)/shard_map/jit(_take)/gather | solution.py:125
  118.2 0.8 multiply_reduce_fusion
  118.9 7.4 %multiply_bitcast_fusion = f32[6,16,128,128]{3,2,0,1:T(8,128)S(1)} fusion(f32[6,128]{1,0:T(8,128)S(1)} %add_rsqrt_fusion, f32[128]{0:T(128)S(1)} %add_rsqrt_fusion.1, bf16[16,128,1536,1]{2,1,0,3:T(8,128)(2,1)} %reshape.156, bf16[6,128,1536]{2,1,0:T(8,128)(2,1)S(1)} %gather_fusion, pred[6]{0:T(512)(128)(4,1)S(1)} %get-tuple-element.7), kind=kOutput, calls=%fused_computation.4 | convolution fusion | flops 4837736448 | bytes 14945798 | tf_op jit(solution)/shard_map/dot_general | solution.py:83
  126.3 3.1 %copy.17 = f32[6,16,128,128]{3,2,1,0:T(8,128)} copy(f32[6,16,128,128]{3,2,0,1:T(8,128)S(1)} %multiply_bitcast_fusion) | data formatting | bytes 12582912 | tf_op jit(solution)/shard_map/mul | solution.py:88
  (33 shorter events, 2.6 us)
Async XLA Ops:
  0.0 8.8 %copy-start = (f32[16,128]{1,0:T(8,128)S(1)}, f32[16,128]{1,0:T(8,128)}, u32[]{:S(2)}) copy-start(f32[16,128]{1,0:T(8,128)} %param.7) | copy-start | bytes 24580
  3.8 4.1 %copy-start.2 = (s32[128]{0:T(128)S(1)}, s32[128]{0:T(128)}, u32[]{:S(2)}) copy-start(s32[128]{0:T(128)} %param.8) | copy-start | bytes 1540
  3.9 4.1 %copy-start.1 = (s32[6,1]{0,1:T(1,128)S(1)}, s32[6,1]{0,1:T(1,128)}, u32[]{:S(2)}) copy-start(s32[6,1]{0,1:T(1,128)} %param.9) | copy-start | bytes 76
  3.9 4.2 %copy-start.3 = (f32[64]{0:T(128)S(1)}, f32[64]{0:T(128)}, u32[]{:S(2)}) copy-start(f32[64]{0:T(128)} %param.6) | copy-start | bytes 772
  3.9 41.9 %all-to-all-start = ((bf16[2,3,2048,128]{3,2,1,0:T(8,128)(2,1)}), bf16[2,3,2048,128]{3,2,1,0:T(8,128)(2,1)S(1)}, u32[]{:S(2)}, u32[]{:S(2)}) async-start(bf16[2,3,2048,128]{3,2,1,0:T(8,128)(2,1)} %pad_maximum_fusion.1), calls=%async_computation | async-start | bytes 6291456 | tf_op jit(solution)/shard_map/all_to_all | solution.py:100
  48.5 54.9 %collective-permute-start = (bf16[128,1536]{1,0:T(8,128)(2,1)S(1)}, bf16[128,1536]{1,0:T(8,128)(2,1)}, u32[]{:S(2)}, u32[]{:S(2)}) collective-permute-start(bf16[128,1536]{1,0:T(8,128)(2,1)S(1)} %copy.11), channel_id=1, source_target_pairs={{0,8},{2,10},{4,12},{6,14},{8,16},{10,18},{12,20},{14,22},{16,24},... | collective-permute-start | bytes 1179656 | tf_op jit(solution)/shard_map/ppermute | solution.py:15
  51.8 55.5 %collective-permute-start.1 = (bf16[128,1536]{1,0:T(8,128)(2,1)S(1)}, bf16[128,1536]{1,0:T(8,128)(2,1)S(1)}, u32[]{:S(2)}, u32[]{:S(2)}) collective-permute-start(bf16[128,1536]{1,0:T(8,128)(2,1)S(1)} %copy.11), channel_id=1, source_target_pairs={{0,4},{2,6},{4,8},{6,10},{8,12},{10,14},{12,16},{14,18},{16,20},{1... | collective-permute-start | bytes 1179656 | tf_op jit(solution)/shard_map/ppermute | solution.py:15
  52.5 55.6 %collective-permute-start.2 = (bf16[128,1536]{1,0:T(8,128)(2,1)S(1)}, bf16[128,1536]{1,0:T(8,128)(2,1)S(1)}, u32[]{:S(2)}, u32[]{:S(2)}) collective-permute-start(bf16[128,1536]{1,0:T(8,128)(2,1)S(1)} %copy.11), channel_id=1, source_target_pairs={{0,2},{2,4},{4,6},{6,8},{8,10},{10,12},{12,14},{14,16},{16,18},{18... | collective-permute-start | bytes 1179656 | tf_op jit(solution)/shard_map/ppermute | solution.py:15
  52.5 56.4 %collective-permute-start.3 = (bf16[128,1536]{1,0:T(8,128)(2,1)S(1)}, bf16[128,1536]{1,0:T(8,128)(2,1)S(1)}, u32[]{:S(2)}, u32[]{:S(2)}) collective-permute-start(bf16[128,1536]{1,0:T(8,128)(2,1)S(1)} %copy.11), channel_id=1, source_target_pairs={{0,254},{2,0},{4,2},{6,4},{8,6},{10,8},{12,10},{14,12},{16,14},{18... | collective-permute-start | bytes 1179656 | tf_op jit(solution)/shard_map/ppermute | solution.py:15
  58.5 51.2 %collective-permute-start.4 = (bf16[128,1536]{1,0:T(8,128)(2,1)S(1)}, bf16[128,1536]{1,0:T(8,128)(2,1)S(1)}, u32[]{:S(2)}, u32[]{:S(2)}) collective-permute-start(bf16[128,1536]{1,0:T(8,128)(2,1)S(1)} %copy.11), channel_id=1, source_target_pairs={{0,252},{2,254},{4,0},{6,2},{8,4},{10,6},{12,8},{14,10},{16,12},{1... | collective-permute-start | bytes 1179656 | tf_op jit(solution)/shard_map/ppermute | solution.py:15
  103.5 11.6 %collective-permute-start.5 = (bf16[128,1536]{1,0:T(8,128)(2,1)S(1)}, bf16[128,1536]{1,0:T(8,128)(2,1)S(1)}, u32[]{:S(2)}, u32[]{:S(2)}) collective-permute-start(bf16[128,1536]{1,0:T(8,128)(2,1)S(1)} %copy.11), channel_id=1, source_target_pairs={{0,248},{2,250},{4,252},{6,254},{8,0},{10,2},{12,4},{14,6},{16,8},... | collective-permute-start | bytes 1179656 | tf_op jit(solution)/shard_map/ppermute | solution.py:15
